TPU v7x, 32 devices: a whole 2x2x4 slice. The times are simulated.
32 devices in a mesh: cls: 8 (over y, x, core), batch: 4 (over z).
Axes of the slice: x: 2, y: 2, z: 4, core: 2. Of those that a mesh axis runs over, the one named last changes fastest.
Arguments:
- features: bfloat16 [4096, 1024], P('batch'), may hold values from -6 to 6
- head_weight: bfloat16 [1024, 1024], P('cls'), may hold values from -0.1875 to 0.1875
- inliers: bfloat16 [8192, 1024], P('cls'), may hold values from -2.5 to 2.5
- outliers: bfloat16 [8192, 1024], P('cls'), may hold values from -2.5 to 2.5
- inlier_counts: int32 [8192], P('cls'), may hold values from 1 to 9
- outlier_counts: int32 [8192], P('cls'), may hold values from 1 to 9
- labels: int32 [4096], P('batch'), may hold values from 0 to 1
Outputs:
- energy: float32 [4096], P('batch')
- head_grad: float32 [1024, 1024], P('cls')
All inputs are finite; a program needn't handle non-finite values.
Results may differ from a plain program's by a relative error of at most 0.0076.
The roundings to bfloat16 on the way count: a program that leaves them out, or rounds other values in their place, can miss the bound.
Values may be sent and summed in bfloat16 or wider, within the bound.
No kernel may reach another device: no remote copies, remote signals or barrier semaphores. Data moves between devices by JAX's collectives and lax.ppermute only.
A program may use at most 64 MiB of HBM per device.

v0:
```python
import jax
import jax.numpy as jnp
from jax import lax
from jax.sharding import PartitionSpec as P

beta = 2.0


def score_rows(queries, patterns, counts):
    log_counts = jnp.log(counts.astype(jnp.float32))
    return (
        beta * jnp.dot(queries, patterns.T, preferred_element_type=jnp.float32)
        + log_counts[None, :]
    )


def split_parts(values):
    high_part = values.astype(jnp.bfloat16)
    low_part = (values - high_part.astype(jnp.float32)).astype(jnp.bfloat16)
    return (high_part, low_part)


def outer_rows(columns, high_part, low_part):
    first = jnp.einsum("qf,qd->fd", columns, high_part, preferred_element_type=jnp.float32)
    return first + jnp.einsum("qf,qd->fd", columns, low_part, preferred_element_type=jnp.float32)


def body(features, head_weight, inliers, outliers, inlier_counts, outlier_counts, labels):
    columns = features
    queries = jnp.dot(
        columns,
        lax.all_gather(head_weight, "cls", axis=0, tiled=True),
        preferred_element_type=jnp.float32,
    ).astype(jnp.bfloat16)
    in_scores = score_rows(queries, inliers, inlier_counts)
    out_scores = score_rows(queries, outliers, outlier_counts)
    in_top, out_top = lax.pmax((jnp.max(in_scores, axis=1), jnp.max(out_scores, axis=1)), "cls")
    in_expon = jnp.exp(in_scores - in_top[:, None])
    out_expon = jnp.exp(out_scores - out_top[:, None])
    in_total, out_total = lax.psum((jnp.sum(in_expon, axis=1), jnp.sum(out_expon, axis=1)), "cls")
    in_sum = jnp.dot(in_expon.astype(jnp.bfloat16), inliers, preferred_element_type=jnp.float32)
    out_sum = jnp.dot(out_expon.astype(jnp.bfloat16), outliers, preferred_element_type=jnp.float32)
    energy = (in_top + jnp.log(in_total) - (out_top + jnp.log(out_total))) / beta
    label_sign = 2.0 * labels.astype(jnp.float32) - 1.0
    slope_term = -label_sign * jax.nn.sigmoid(-label_sign * energy)
    query_grad = slope_term[:, None] * (in_sum / in_total[:, None] - out_sum / out_total[:, None])
    grad_high, grad_low = split_parts(query_grad)
    columns = features
    partial_value = lax.psum_scatter(
        outer_rows(columns, grad_high, grad_low), "cls", scatter_dimension=0, tiled=True
    )
    head_grad = lax.psum(partial_value, "batch")
    return (energy, head_grad)


def solution(mesh):
    placed = (
        P("batch", None),
        P("cls", None),
        P("cls", None),
        P("cls", None),
        P("cls"),
        P("cls"),
        P("batch"),
    )
    return jax.shard_map(
        body, mesh=mesh, in_specs=placed, out_specs=(P("batch"), P("cls", None)), check_vma=False
    )
```

profile of v0, /device:TPU:0, one launch (start us, length us, event | category | flops | bytes accessed | tf_op | source)
XLA Modules:
  0.0 203.2 jit_solution(14456666442789482762)
XLA Ops:
  7.2 0.0 copy-start
  7.2 0.0 all-gather.2.cloned.1.call-start
  7.2 0.7 all-gather.2.cloned.1.call-update
  7.9 0.0 reduce-scatter.2.cloned.1.call-start
  8.0 0.7 convert_log_fusion.1
  8.7 0.7 convert_log_fusion
  9.3 31.1 %all-gather.2.cloned.1.call-done = bf16[1024,1024]{1,0:T(8,128)(2,1)} async-done(((bf16[128,1024]{1,0:T(8,128)(2,1)}), bf16[1024,1024]{1,0:T(8,128)(2,1)}) %all-gather.2.cloned.1.call-update) | async-done | bytes 2097168 | tf_op jit(solution)/shard_map/all_gather | solution.py:32
  40.4 4.1 %convolution_convert_fusion = bf16[1024,1024]{1,0:T(8,128)(2,1)S(1)} fusion(bf16[1024,1024]{1,0:T(8,128)(2,1)S(1)} %copy-done, bf16[1024,1024]{1,0:T(8,128)(2,1)} %all-gather.2.cloned.1.call-done), kind=kOutput, calls=%fused_computation.22 | convolution fusion | flops 2148532224 | bytes 6291456 | tf_op jit(solution)/shard_map/dot_general | solution.py:30
  44.5 4.3 %fusion.1 = (f32[1024]{0:T(1024)S(1)}, f32[1024,1024]{0,1:T(8,128)}) fusion(f32[1024]{0:T(1024)S(1)} %convert_log_fusion, bf16[1024,1024]{1,0:T(8,128)(2,1)S(1)} %convolution_convert_fusion, bf16[1024,1024]{1,0:T(8,128)(2,1)S(1)} %copy-done.4), kind=kOutput, calls=%fused_computation.8 | convolution fusion | flops 2150628352 | bytes 8396800 | tf_op jit(solution)/shard_map/dot_general | solution.py:12
  48.8 4.3 %fusion = (f32[1024]{0:T(1024)S(1)}, f32[1024,1024]{0,1:T(8,128)}) fusion(f32[1024]{0:T(1024)S(1)} %convert_log_fusion.1, bf16[1024,1024]{1,0:T(8,128)(2,1)S(1)} %convolution_convert_fusion, bf16[1024,1024]{1,0:T(8,128)(2,1)S(1)} %copy-done.5), kind=kOutput, calls=%fused_computation.7 | convolution fusion | flops 2150628352 | bytes 8396800 | tf_op jit(solution)/shard_map/dot_general | solution.py:12
  53.2 13.3 %all-reduce.1 = (f32[1024]{0:T(1024)S(1)}, f32[1024]{0:T(1024)S(1)}) all-reduce(f32[1024]{0:T(1024)S(1)} %get-tuple-element.10, f32[1024]{0:T(1024)S(1)} %get-tuple-element.12), channel_id=1, replica_groups=mesh['cls'=8,'batch'=4] {'cls'}, use_global_device_ids=true, to_apply=%region_5.0 | all-reduce | flops 2048 | bytes 16384 | tf_op jit(solution)/shard_map/pmax | solution.py:37
  66.5 7.5 %fusion.6 = f32[1024,1024]{1,0:T(8,128)} fusion(bf16[1024,1024]{1,0:T(8,128)(2,1)} %param.10, f32[1024,1024]{0,1:T(8,128)} %get-tuple-element.11, f32[1024]{0:T(1024)S(1)} %get-tuple-element.6, f32[1024]{0:T(1024)S(1)} %convert_log_fusion), kind=kOutput, calls=%fused_computation.13 | convolution fusion | flops 2151677952 | bytes 10493952 | tf_op jit(solution)/shard_map/dot_general | solution.py:42
  74.0 1.9 fusion.3
  75.9 12.2 %all-reduce = (f32[1024]{0:T(1024)S(1)}, f32[1024]{0:T(1024)S(1)}) all-reduce(f32[1024]{0:T(1024)S(1)} %get-tuple-element.15, f32[1024]{0:T(1024)S(1)} %get-tuple-element.14), channel_id=1, replica_groups=mesh['cls'=8,'batch'=4] {'cls'}, use_global_device_ids=true, to_apply=%region_7.0 | all-reduce | flops 2048 | bytes 16384 | tf_op jit(solution)/shard_map/psum | solution.py:40
  88.2 0.6 divide_multiply_fusion
  88.8 6.9 %subtract_multiply_fusion = f32[1024,1024]{1,0:T(8,128)S(1)} fusion(f32[1024,1024]{1,0:T(8,128)} %fusion.6, f32[1024]{0:T(1024)S(1)} %get-tuple-element.4, f32[1024]{0:T(1024)S(1)} %get-tuple-element.5, f32[1024]{0:T(1024)S(1)} %get-tuple-element.8, bf16[1024,1024]{1,0:T(8,128)(2,1)} %param.9, f32[1024,1024]{0,1:T(8,128)} %get-tuple-element.13, ...), kind=kOutput, calls=%fused_computation.2 | convolution fusion | flops 2155872256 | bytes 14700544 | tf_op jit(solution)/shard_map/dot_general | solution.py:41
  95.7 2.4 %fusion.20 = f32[1024,1024]{1,0:T(8,128)S(1)} fusion(bf16[1024,1024]{1,0:T(8,128)(2,1)S(1)} %copy-done, f32[1024,1024]{1,0:T(8,128)S(1)} %subtract_multiply_fusion), kind=kOutput, calls=%fused_computation.24 | convolution fusion | flops 2148532224 | bytes 10485760 | tf_op jit(solution)/shard_map/qf,qd->fd/dot_general | solution.py:24
  98.1 4.3 %add_bitcast_fusion = f32[1024,1024]{0,1:T(8,128)} fusion(f32[1024,1024]{1,0:T(8,128)S(1)} %fusion.20, bf16[1024,1024]{1,0:T(8,128)(2,1)S(1)} %copy-done, f32[1024,1024]{1,0:T(8,128)S(1)} %subtract_multiply_fusion), kind=kOutput, calls=%fused_computation | convolution fusion | flops 2152726528 | bytes 14680064 | tf_op jit(solution)/shard_map/qf,qd->fd/dot_general | solution.py:25
  102.4 0.0 reduce-scatter.2.cloned.1.call-update
  102.4 0.0 all-reduce.4.cloned.1.call-start
  102.4 51.3 %reduce-scatter.2.cloned.1.call-done = f32[128,1024]{0,1:T(8,128)} async-done(((f32[1024,1024]{0,1:T(8,128)}), f32[128,1024]{0,1:T(8,128)}) %reduce-scatter.2.cloned.1.call-update) | async-done | bytes 524304 | tf_op jit(solution)/shard_map/reduce_scatter | solution.py:49
  153.7 0.0 all-reduce.4.cloned.1.call-update
  153.7 40.9 %all-reduce.4.cloned.1.call-done = f32[128,1024]{0,1:T(8,128)} async-done(((f32[128,1024]{0,1:T(8,128)}), f32[128,1024]{0,1:T(8,128)}) %all-reduce.4.cloned.1.call-update) | async-done | bytes 524304 | tf_op jit(solution)/shard_map/psum | solution.py:52
  194.7 2.0 %copy.9 = f32[128,1024]{1,0:T(8,128)} copy(f32[128,1024]{0,1:T(8,128)} %all-reduce.4.cloned.1.call-done) | data formatting | bytes 1048576
  (11 shorter events, 0.0 us)
Async XLA Ops:
  7.2 33.2 %copy-start = (bf16[1024,1024]{1,0:T(8,128)(2,1)S(1)}, bf16[1024,1024]{1,0:T(8,128)(2,1)}, u32[]{:S(2)}) copy-start(bf16[1024,1024]{1,0:T(8,128)(2,1)} %param.7) | copy-start | bytes 6291460
  7.2 33.2 %all-gather.2.cloned.1.call-start = ((), (), s32[]{:S(2)}) async-start(), calls=%async_computation.1 | async-start | bytes 2359296 | tf_op jit(solution)/shard_map/all_gather | solution.py:32
  7.9 145.8 %reduce-scatter.2.cloned.1.call-start = ((), (), s32[]{:S(2)}) async-start(), calls=%async_computation.2 | async-start | bytes 4718592 | tf_op jit(solution)/shard_map/reduce_scatter | solution.py:49
  40.4 4.1 %copy-start.4 = (bf16[1024,1024]{1,0:T(8,128)(2,1)S(1)}, bf16[1024,1024]{1,0:T(8,128)(2,1)}, u32[]{:S(2)}) copy-start(bf16[1024,1024]{1,0:T(8,128)(2,1)} %param.10) | copy-start | bytes 6291460
  44.5 4.3 %copy-start.5 = (bf16[1024,1024]{1,0:T(8,128)(2,1)S(1)}, bf16[1024,1024]{1,0:T(8,128)(2,1)}, u32[]{:S(2)}) copy-start(bf16[1024,1024]{1,0:T(8,128)(2,1)} %param.9) | copy-start | bytes 6291460
  66.5 7.5 %copy-start.1 = (f32[1024,1024]{0,1:T(8,128)S(1)}, f32[1024,1024]{0,1:T(8,128)}, u32[]{:S(2)}) copy-start(f32[1024,1024]{0,1:T(8,128)} %get-tuple-element.13) | copy-start | bytes 12582916
  66.5 7.5 %copy-start.2 = (f32[1024,1024]{0,1:T(8,128)S(1)}, f32[1024,1024]{0,1:T(8,128)}, u32[]{:S(2)}) copy-start(f32[1024,1024]{0,1:T(8,128)} %get-tuple-element.11) | copy-start | bytes 12582916
  74.0 14.2 %copy-start.3 = (s32[1024]{0:T(1024)S(1)}, s32[1024]{0:T(1024)}, u32[]{:S(2)}) copy-start(s32[1024]{0:T(1024)} %param.13) | copy-start | bytes 12292
  102.4 92.3 %all-reduce.4.cloned.1.call-start = ((), (), s32[]{:S(2)}) async-start(), calls=%async_computation.3 | async-start | bytes 1048576 | tf_op jit(solution)/shard_map/psum | solution.py:52
Sparse Core Ops, SparseCore 0:
  9.9 30.4 all-gather.1
  102.5 51.1 reduce-scatter.1
  156.1 38.5 all-reduce.3
where the time goes:
time: 204 us; the launch traced here: 203 us
  waiting for transfers between devices  124 us (61%)
  matrix products  33.8 us (17%)
  blocking collectives  25.5 us (12%)
  between operations  13.8 us (7%)
  other arithmetic  3.94 us (2%)
  local copies, waits for them, and re-layouts  2.07 us (1%)
    reduce_scatter x1, waiting for transfers between devices, body(): lax.psum_scatter(outer_rows(columns, grad_high, grad_low), 'cls', scatter...  51.3 us
    psum x1, waiting for transfers between devices, body(): head_grad = lax.psum(partial_value, 'batch')  40.9 us
    all_gather x1, waiting for transfers between devices, body(): lax.all_gather(head_weight, 'cls', axis=0, tiled=True)  31.1 us
    pmax x1, blocking collectives, body(): lax.pmax((jnp.max(in_scores, axis=1), jnp.max(out_scores, axis=1)), 'cls')  13.3 us
    psum x1, blocking collectives, body(): lax.psum((jnp.sum(in_expon, axis=1), jnp.sum(out_expon, axis=1)), 'cls')  12.2 us
    dot_general x2, matrix products, score_rows(): jnp.dot(queries, patterns.T, preferred_element_type=jnp.float32)  8.65 us
    dot_general x1, matrix products, body(): jnp.dot(out_expon.astype(jnp.bfloat16), outliers, preferred_element_type=...  7.48 us
    dot_general x1, matrix products, body(): jnp.dot(in_expon.astype(jnp.bfloat16), inliers, preferred_element_type=jn...  6.85 us
  transfers between devices with their start and end apart: 3, of which 3 were waited for; matrix products, arithmetic and copies ran while one was open for 1% of the time, Pallas kernels for 0%

commit v1 on v0

--- a/solution.py
+++ b/solution.py
@@ -4,6 +4,22 @@
 from jax.sharding import PartitionSpec as P
 
 beta = 2.0
+
+
+def prepare_body(v0):
+    group_axis = "cls"
+    met_up = lax.psum(1, group_axis)
+    frame_out = lax.axis_index(group_axis)
+    new, y1, item_now = (met_up, frame_out, v0.shape[0])
+    plain, carry = (v0, 1)
+    while carry < new:
+        res = range(new)
+        a_next = map(lambda k: (k, (k - carry) % new), res)
+        o_now = list(a_next)
+        d_next = lax.ppermute(plain, group_axis, o_now)
+        plain = jnp.concatenate([plain, d_next], 0)
+        carry = 2 * carry
+    return jnp.roll(plain, y1 * item_now, 0)
 
 
 def score_rows(queries, patterns, counts):
@@ -28,9 +44,7 @@
 def body(features, head_weight, inliers, outliers, inlier_counts, outlier_counts, labels):
     columns = features
     queries = jnp.dot(
-        columns,
-        lax.all_gather(head_weight, "cls", axis=0, tiled=True),
-        preferred_element_type=jnp.float32,
+        columns, prepare_body(head_weight), preferred_element_type=jnp.float32
     ).astype(jnp.bfloat16)
     in_scores = score_rows(queries, inliers, inlier_counts)
     out_scores = score_rows(queries, outliers, outlier_counts)

time: 204 us -> 221 us (1.083)
  waiting for transfers between devices: 124 us -> 131 us
  starting transfers between devices: 0.12 us -> 4.75 us
  local copies, waits for them, and re-layouts: 2.07 us -> 5.76 us
  other arithmetic: 3.94 us -> 6.92 us
    ppermute x0 -> x3, waiting for transfers between devices: none -> 39.7 us  [prepare_body(): d_next = lax.ppermute(plain, group_axis, o_now)]
    all_gather x1 -> x0, waiting for transfers between devices: 31.1 us -> none  [body(): lax.all_gather(head_weight, 'cls', axis=0, tiled=True)]
    ppermute x0 -> x3, starting transfers between devices: none -> 4.67 us  [prepare_body(): d_next = lax.ppermute(plain, group_axis, o_now)]
    concatenate x0 -> x2, other arithmetic: none -> 2.99 us  [prepare_body(): plain = jnp.concatenate([plain, d_next], 0)]
    unnamed x13 -> x22, local copies, waits for them, and re-layouts: 2.07 us -> 4.47 us
  transfers between devices with their start and end apart: 3 -> 5, of which waited for: 3 -> 5; matrix products, arithmetic and copies ran while one was open for 1% -> 1% of each run, Pallas kernels for 0% -> 0%
where the time goes in v1:
time: 221 us
  waiting for transfers between devices  131 us (59%)
  matrix products  32.6 us (15%)
  blocking collectives  25.6 us (12%)
  between operations  14.2 us (6%)
  other arithmetic  6.92 us (3%)
  local copies, waits for them, and re-layouts  5.76 us (3%)
  starting transfers between devices  4.75 us (2%)
    reduce_scatter x1, waiting for transfers between devices, body(): lax.psum_scatter(outer_rows(columns, grad_high, grad_low), 'cls', scatter...  50.5 us
    psum x1, waiting for transfers between devices, body(): head_grad = lax.psum(partial_value, 'batch')  40.9 us
    ppermute x3, waiting for transfers between devices, prepare_body(): d_next = lax.ppermute(plain, group_axis, o_now)  39.7 us
    pmax x1, blocking collectives, body(): lax.pmax((jnp.max(in_scores, axis=1), jnp.max(out_scores, axis=1)), 'cls')  13.3 us
    psum x1, blocking collectives, body(): lax.psum((jnp.sum(in_expon, axis=1), jnp.sum(out_expon, axis=1)), 'cls')  12.3 us
    dot_general x2, matrix products, score_rows(): jnp.dot(queries, patterns.T, preferred_element_type=jnp.float32)  8.58 us
    dot_general x1, matrix products, body(): jnp.dot(out_expon.astype(jnp.bfloat16), outliers, preferred_element_type=...  7.49 us
    dot_general x1, matrix products, body(): jnp.dot(in_expon.astype(jnp.bfloat16), inliers, preferred_element_type=jn...  7.08 us
  transfers between devices with their start and end apart: 5, of which 5 were waited for; matrix products, arithmetic and copies ran while one was open for 1% of the time, Pallas kernels for 0%

profile of v1, /device:TPU:0, one launch (start us, length us, event | category | flops | bytes accessed | tf_op | source)
XLA Modules:
  0.0 221.1 jit_solution(3358176658697701278)
XLA Ops:
  7.2 3.4 %collective-permute-start = (bf16[128,1024]{1,0:T(8,128)(2,1)}, bf16[128,1024]{1,0:T(8,128)(2,1)S(1)}, u32[]{:S(2)}, u32[]{:S(2)}) collective-permute-start(bf16[128,1024]{1,0:T(8,128)(2,1)} %param.8), channel_id=1, source_target_pairs={{0,28},{4,0},{8,4},{12,8},{16,12},{20,16},{24,20},{28,24},{1,29},{... | collective-permute-start | bytes 786440 | tf_op jit(solution)/shard_map/ppermute | solution.py:19
  10.7 4.2 %collective-permute-done = bf16[128,1024]{1,0:T(8,128)(2,1)S(1)} collective-permute-done((bf16[128,1024]{1,0:T(8,128)(2,1)}, bf16[128,1024]{1,0:T(8,128)(2,1)S(1)}, u32[]{:S(2)}, u32[]{:S(2)}) %collective-permute-start) | collective-permute-done | bytes 262176 | tf_op jit(solution)/shard_map/ppermute | solution.py:19
  14.9 1.0 pad_maximum_fusion.1
  16.5 13.7 %collective-permute-done.1 = bf16[256,1024]{1,0:T(8,128)(2,1)S(1)} collective-permute-done((bf16[256,1024]{1,0:T(8,128)(2,1)S(1)}, bf16[256,1024]{1,0:T(8,128)(2,1)S(1)}, u32[]{:S(2)}, u32[]{:S(2)}) %collective-permute-start.1) | collective-permute-done | bytes 524320 | tf_op jit(solution)/shard_map/ppermute | solution.py:19
  30.1 2.0 pad_maximum_fusion
  32.8 1.0 constant_dynamic-update-slice_fusion.7
  33.7 0.7 convert_log_fusion.1
  34.4 0.7 convert_log_fusion
  35.2 21.9 %collective-permute-done.2 = bf16[512,1024]{1,0:T(8,128)(2,1)} collective-permute-done((bf16[512,1024]{1,0:T(8,128)(2,1)}, bf16[512,1024]{1,0:T(8,128)(2,1)}, u32[]{:S(2)}, u32[]{:S(2)}) %collective-permute-start.2) | collective-permute-done | bytes 1048608 | tf_op jit(solution)/shard_map/ppermute | solution.py:19
  57.1 1.3 constant_dynamic-update-slice_fusion.4
  58.5 1.3 constant_dynamic-update-slice_fusion
  59.8 2.4 %fusion.21 = bf16[1024,1024]{1,0:T(8,128)(2,1)S(1)} fusion(bf16[1024,1024]{1,0:T(8,128)(2,1)S(1)} %copy-done, bf16[2048,1024]{1,0:T(8,128)(2,1)S(1)} %constant_dynamic-update-slice_fusion, s32[]{:T(128)S(6)} %select_n.14), kind=kOutput, calls=%fused_computation.24 | convolution fusion | flops 2148532224 | bytes 6291460 | tf_op jit(solution)/shard_map/dot_general | solution.py:46
  62.2 4.3 %fusion.1 = (f32[1024]{0:T(1024)S(1)}, f32[1024,1024]{0,1:T(8,128)}) fusion(f32[1024]{0:T(1024)S(1)} %convert_log_fusion, bf16[1024,1024]{1,0:T(8,128)(2,1)S(1)} %copy-done.5, bf16[1024,1024]{1,0:T(8,128)(2,1)S(1)} %fusion.21), kind=kOutput, calls=%fused_computation.8 | convolution fusion | flops 2150628352 | bytes 8396800 | tf_op jit(solution)/shard_map/dot_general | solution.py:28
  66.5 4.3 %fusion = (f32[1024]{0:T(1024)S(1)}, f32[1024,1024]{0,1:T(8,128)}) fusion(f32[1024]{0:T(1024)S(1)} %convert_log_fusion.1, bf16[1024,1024]{1,0:T(8,128)(2,1)S(1)} %copy-done.6, bf16[1024,1024]{1,0:T(8,128)(2,1)S(1)} %fusion.21), kind=kOutput, calls=%fused_computation.7 | convolution fusion | flops 2150628352 | bytes 8396800 | tf_op jit(solution)/shard_map/dot_general | solution.py:28
  70.8 13.3 %all-reduce.1 = (f32[1024]{0:T(1024)S(1)}, f32[1024]{0:T(1024)S(1)}) all-reduce(f32[1024]{0:T(1024)S(1)} %get-tuple-element.10, f32[1024]{0:T(1024)S(1)} %get-tuple-element.12), channel_id=1, replica_groups=mesh['cls'=8,'batch'=4] {'cls'}, use_global_device_ids=true, to_apply=%region_5.6 | all-reduce | flops 2048 | bytes 16384 | tf_op jit(solution)/shard_map/pmax | solution.py:51
  84.2 7.5 %fusion.6 = f32[1024,1024]{1,0:T(8,128)} fusion(bf16[1024,1024]{1,0:T(8,128)(2,1)} %param.10, f32[1024,1024]{0,1:T(8,128)} %get-tuple-element.11, f32[1024]{0:T(1024)S(1)} %get-tuple-element.6, f32[1024]{0:T(1024)S(1)} %convert_log_fusion), kind=kOutput, calls=%fused_computation.13 | convolution fusion | flops 2151677952 | bytes 10493952 | tf_op jit(solution)/shard_map/dot_general | solution.py:56
  91.7 1.9 fusion.3
  93.6 12.3 %all-reduce = (f32[1024]{0:T(1024)S(1)}, f32[1024]{0:T(1024)S(1)}) all-reduce(f32[1024]{0:T(1024)S(1)} %get-tuple-element.15, f32[1024]{0:T(1024)S(1)} %get-tuple-element.14), channel_id=1, replica_groups=mesh['cls'=8,'batch'=4] {'cls'}, use_global_device_ids=true, to_apply=%region_7.8 | all-reduce | flops 2048 | bytes 16384 | tf_op jit(solution)/shard_map/psum | solution.py:54
  106.5 7.1 %subtract_multiply_fusion = f32[1024,1024]{1,0:T(8,128)S(1)} fusion(f32[1024,1024]{1,0:T(8,128)} %fusion.6, f32[1024]{0:T(1024)S(1)} %get-tuple-element.4, f32[1024]{0:T(1024)S(1)} %get-tuple-element.5, f32[1024]{0:T(1024)S(1)} %get-tuple-element.8, bf16[1024,1024]{1,0:T(8,128)(2,1)} %param.9, f32[1024,1024]{0,1:T(8,128)} %get-tuple-element.13, ...), kind=kOutput, calls=%fused_computation.2 | convolution fusion | flops 2155872256 | bytes 14700544 | tf_op jit(solution)/shard_map/dot_general | solution.py:55
  113.6 2.5 %fusion.25 = f32[1024,1024]{1,0:T(8,128)S(1)} fusion(bf16[1024,1024]{1,0:T(8,128)(2,1)S(1)} %copy-done, f32[1024,1024]{1,0:T(8,128)S(1)} %subtract_multiply_fusion), kind=kOutput, calls=%fused_computation.27 | convolution fusion | flops 2148532224 | bytes 10485760 | tf_op jit(solution)/shard_map/qf,qd->fd/dot_general | solution.py:40
  116.1 4.5 %add_bitcast_fusion = f32[1024,1024]{0,1:T(8,128)} fusion(f32[1024,1024]{1,0:T(8,128)S(1)} %fusion.25, bf16[1024,1024]{1,0:T(8,128)(2,1)S(1)} %copy-done, f32[1024,1024]{1,0:T(8,128)S(1)} %subtract_multiply_fusion), kind=kOutput, calls=%fused_computation | convolution fusion | flops 2152726528 | bytes 14680064 | tf_op jit(solution)/shard_map/qf,qd->fd/dot_general | solution.py:41
  120.7 50.5 %reduce-scatter.2.cloned.1.call-done = f32[128,1024]{0,1:T(8,128)} async-done(((f32[1024,1024]{0,1:T(8,128)}), f32[128,1024]{0,1:T(8,128)}) %reduce-scatter.2.cloned.1.call-update) | async-done | bytes 524304 | tf_op jit(solution)/shard_map/reduce_scatter | solution.py:63
  171.3 40.9 %all-reduce.4.cloned.1.call-done = f32[128,1024]{0,1:T(8,128)} async-done(((f32[128,1024]{0,1:T(8,128)}), f32[128,1024]{0,1:T(8,128)}) %all-reduce.4.cloned.1.call-update) | async-done | bytes 524304 | tf_op jit(solution)/shard_map/psum | solution.py:66
  212.2 2.0 copy.9
  (26 shorter events, 2.1 us)
Async XLA Ops:
  7.2 52.6 %copy-start = (bf16[1024,1024]{1,0:T(8,128)(2,1)S(1)}, bf16[1024,1024]{1,0:T(8,128)(2,1)}, u32[]{:S(2)}) copy-start(bf16[1024,1024]{1,0:T(8,128)(2,1)} %param.7) | copy-start | bytes 6291460
  7.2 51.2 %copy-start.3 = (bf16[128,1024]{1,0:T(8,128)(2,1)S(1)}, bf16[128,1024]{1,0:T(8,128)(2,1)}, u32[]{:S(2)}) copy-start(bf16[128,1024]{1,0:T(8,128)(2,1)} %param.8) | copy-start | bytes 786436
  7.2 164.1 %reduce-scatter.2.cloned.1.call-start = ((), (), s32[]{:S(2)}) async-start(), calls=%async_computation.1 | async-start | bytes 4718592 | tf_op jit(solution)/shard_map/reduce_scatter | solution.py:63
  7.2 7.6 %collective-permute-start = (bf16[128,1024]{1,0:T(8,128)(2,1)}, bf16[128,1024]{1,0:T(8,128)(2,1)S(1)}, u32[]{:S(2)}, u32[]{:S(2)}) collective-permute-start(bf16[128,1024]{1,0:T(8,128)(2,1)} %param.8), channel_id=1, source_target_pairs={{0,28},{4,0},{8,4},{12,8},{16,12},{20,16},{24,20},{28,24},{1,29},{... | collective-permute-start | bytes 786440 | tf_op jit(solution)/shard_map/ppermute | solution.py:19
  15.8 14.3 %collective-permute-start.1 = (bf16[256,1024]{1,0:T(8,128)(2,1)S(1)}, bf16[256,1024]{1,0:T(8,128)(2,1)S(1)}, u32[]{:S(2)}, u32[]{:S(2)}) collective-permute-start(bf16[256,1024]{1,0:T(8,128)(2,1)S(1)} %pad_maximum_fusion.1), channel_id=1, source_target_pairs={{0,24},{4,28},{8,0},{12,4},{16,8},{20,12},{24,16},{28,20},{1,25},{... | collective-permute-start | bytes 1572872 | tf_op jit(solution)/shard_map/ppermute | solution.py:19
  32.1 24.9 %collective-permute-start.2 = (bf16[512,1024]{1,0:T(8,128)(2,1)}, bf16[512,1024]{1,0:T(8,128)(2,1)}, u32[]{:S(2)}, u32[]{:S(2)}) collective-permute-start(bf16[512,1024]{1,0:T(8,128)(2,1)} %pad_maximum_fusion), channel_id=1, source_target_pairs={{0,16},{4,20},{8,24},{12,28},{16,0},{20,4},{24,8},{28,12},{1,17},{... | collective-permute-start | bytes 3145736 | tf_op jit(solution)/shard_map/ppermute | solution.py:19
  59.8 2.4 %copy-start.5 = (bf16[1024,1024]{1,0:T(8,128)(2,1)S(1)}, bf16[1024,1024]{1,0:T(8,128)(2,1)}, u32[]{:S(2)}) copy-start(bf16[1024,1024]{1,0:T(8,128)(2,1)} %param.10) | copy-start | bytes 6291460
  62.2 4.3 %copy-start.6 = (bf16[1024,1024]{1,0:T(8,128)(2,1)S(1)}, bf16[1024,1024]{1,0:T(8,128)(2,1)}, u32[]{:S(2)}) copy-start(bf16[1024,1024]{1,0:T(8,128)(2,1)} %param.9) | copy-start | bytes 6291460
  84.1 7.5 %copy-start.1 = (f32[1024,1024]{0,1:T(8,128)S(1)}, f32[1024,1024]{0,1:T(8,128)}, u32[]{:S(2)}) copy-start(f32[1024,1024]{0,1:T(8,128)} %get-tuple-element.13) | copy-start | bytes 12582916
  84.2 7.5 %copy-start.2 = (f32[1024,1024]{0,1:T(8,128)S(1)}, f32[1024,1024]{0,1:T(8,128)}, u32[]{:S(2)}) copy-start(f32[1024,1024]{0,1:T(8,128)} %get-tuple-element.11) | copy-start | bytes 12582916
  91.7 14.3 %copy-start.4 = (s32[1024]{0:T(1024)S(1)}, s32[1024]{0:T(1024)}, u32[]{:S(2)}) copy-start(s32[1024]{0:T(1024)} %param.13) | copy-start | bytes 12292
  120.7 91.5 %all-reduce.4.cloned.1.call-start = ((), (), s32[]{:S(2)}) async-start(), calls=%async_computation.2 | async-start | bytes 1048576 | tf_op jit(solution)/shard_map/psum | solution.py:66
Sparse Core Ops, SparseCore 0:
  120.8 50.4 reduce-scatter.1
  173.6 38.5 all-reduce.3
